TPU v7x, 256 devices: a whole 4x4x8 slice. The times are simulated.
256 devices in a mesh: spec: 16 (over x, z_lo, core), neuron: 16 (over z_hi, y).
Axes of the slice: x: 4, y: 4, z: 8 (z_hi: 4, z_lo: 2; z = z_hi * 2 + z_lo), core: 2. Of those that a mesh axis runs over, the one named last changes fastest.
Arguments:
- center: float32 [128, 8192], P('spec', 'neuron'), may hold values from -6 to 6
- radius: float32 [128, 8192], P('spec', 'neuron'), may hold values from 0.002 to 0.02
- weight: float32 [4096, 8192], P('neuron'), may hold values from -0.0625 to 0.0625
- bias: float32 [4096], P('neuron'), may hold values from -3 to 3
- out_weight: float32 [1000, 4096], P(None, 'neuron'), may hold values from -0.09375 to 0.09375
- masks: int32 [128, 4096], P(None, 'neuron'), may hold values from 0 to 2
- image_labels: int32 [128], replicated, may hold values from 0 to 999
- runner_up: int32 [8192], P('spec'), may hold values from 0 to 999
- spec_image: int32 [8192], P('spec'), may hold values from 0 to 127
Outputs:
- input_coeffs: float32 [8192, 8192], P('spec', 'neuron')
- margin_bounds: float32 [8192], P('spec')
All inputs are finite; a program needn't handle non-finite values.
Results may differ from a plain program's by a relative error of at most 0.000098.
Values sent between devices are 32-bit elements; how exact they have to be, the bound alone decides.
A program may use at most 128 MiB of HBM per device.

v0:
```python
import jax
import jax.numpy as jnp
from jax import lax
from jax.sharding import PartitionSpec as P


def relax(pre_center, pre_radius, masks):
    upper = pre_center + pre_radius
    lower = pre_center - pre_radius
    slope = jnp.clip(upper / (upper - lower), 0.0, 1.0)
    slopes = jnp.where(
        masks == 1, jnp.ones_like(slope), jnp.where(masks == 2, slope, jnp.zeros_like(slope))
    )
    offsets = jnp.where(masks == 2, slope * lower, jnp.zeros_like(slope))
    return (slopes, offsets)


def interval(center_full, radius_full, weight, bias, masks):
    highest = lax.Precision.HIGHEST
    dims = (((1,), (1,)), ((), ()))
    pre_center = lax.dot_general(center_full, weight, dims, precision=highest) + bias
    pre_radius = lax.dot_general(radius_full, jnp.abs(weight), dims, precision=highest)
    return relax(pre_center, pre_radius, masks)


def local(center, radius, weight, bias, out_weight, masks, image_labels, runner_up, spec_image):
    highest = lax.Precision.HIGHEST
    center_all, radius_all = (
        lax.all_gather(center, "spec", axis=0, tiled=True),
        lax.all_gather(radius, "spec", axis=0, tiled=True),
    )
    center_full, radius_full = (
        lax.all_gather(center_all, "neuron", axis=1, tiled=True),
        lax.all_gather(radius_all, "neuron", axis=1, tiled=True),
    )
    slopes_all, offsets_all = interval(center_full, radius_full, weight, bias, masks)
    true_class = jnp.take(image_labels, spec_image, axis=0)
    spec_coeff = jnp.take(out_weight, true_class, axis=0) - jnp.take(out_weight, runner_up, axis=0)
    scaled = spec_coeff * jnp.take(slopes_all, spec_image, axis=0)
    offset_rows = jnp.take(offsets_all, spec_image, axis=0)
    relax_part = -jnp.sum(jnp.minimum(spec_coeff, 0.0) * offset_rows, axis=1) + jnp.sum(
        scaled * bias, axis=1
    )
    input_coeffs = lax.psum_scatter(
        lax.dot_general(weight, scaled, (((0,), (1,)), ((), ())), precision=highest),
        "neuron",
        scatter_dimension=0,
        tiled=True,
    ).T
    center_rows = jnp.take(center_all, spec_image, axis=0)
    radius_rows = jnp.take(radius_all, spec_image, axis=0)
    input_part = jnp.sum(input_coeffs * center_rows - jnp.abs(input_coeffs) * radius_rows, axis=1)
    margin_bounds = lax.psum(input_part + relax_part, "neuron")
    return (input_coeffs, margin_bounds)


def solution(mesh):
    return jax.shard_map(
        local,
        mesh=mesh,
        in_specs=(
            P("spec", "neuron"),
            P("spec", "neuron"),
            P("neuron", None),
            P("neuron"),
            P(None, "neuron"),
            P(None, "neuron"),
            P(),
            P("spec"),
            P("spec"),
        ),
        out_specs=(P("spec", "neuron"), P("spec")),
        check_vma=False,
    )
```

profile of v0, /device:TPU:2, one launch (start us, length us, event | category | flops | bytes accessed | tf_op | source)
XLA Modules:
  0.0 480.1 jit_solution(12256146682107178975)
XLA Ops:
  7.2 0.0 copy-start
  7.2 0.0 copy-start.4
  7.2 0.0 all-gather.5.cloned.1.call-start
  7.2 20.5 %all_gather.14 = f32[128,512]{1,0:T(8,128)} all-gather(f32[8,512]{1,0:T(8,128)} %param.16), channel_id=1, replica_groups=mesh['spec'=16,'neuron'=16] {'spec'}, dimensions={0}, use_global_device_ids=true | all-gather | bytes 278528 | tf_op jit(solution)/shard_map/all_gather | solution.py:30
  27.8 0.0 all-gather.5.cloned.1.call-update
  27.8 0.0 all-gather.3.cloned.1.call-start
  27.8 19.1 %all_gather.12 = f32[128,512]{1,0:T(8,128)} all-gather(f32[8,512]{1,0:T(8,128)} %param.15), channel_id=1, replica_groups=mesh['spec'=16,'neuron'=16] {'spec'}, dimensions={0}, use_global_device_ids=true | all-gather | bytes 278528 | tf_op jit(solution)/shard_map/all_gather | solution.py:29
  46.9 0.0 all-gather.3.cloned.1.call-update
  47.0 0.0 reduce-scatter.2.cloned.1.call-start
  47.0 0.7 compare_select_fusion.2
  47.7 3.4 gather_fusion
  51.1 0.7 compare_and_fusion.1
  51.8 0.0 copy-done
  51.9 1.6 gather_fusion.1
  53.4 0.7 compare_select_fusion
  54.1 0.0 copy-start.3
  54.1 0.0 copy-start.5
  54.2 1.8 gather_fusion.2
  55.9 0.0 copy-done.4
  55.9 50.1 %all-gather.5.cloned.1.call-done = f32[128,8192]{1,0:T(8,128)} async-done(((f32[128,512]{1,0:T(8,128)}), f32[128,8192]{1,0:T(8,128)}) %all-gather.5.cloned.1.call-update) | async-done | bytes 4194320 | tf_op jit(solution)/shard_map/all_gather | solution.py:34
  106.0 13.0 %fusion = f32[128,256]{1,0:T(8,128)S(1)} fusion(f32[128,8192]{1,0:T(8,128)} %all-gather.5.cloned.1.call-done, f32[256,8192]{1,0:T(8,128)} %param.17), kind=kOutput, calls=%fused_computation.8 | convolution fusion | flops 3223322624 | bytes 12713984 | tf_op jit(solution)/shard_map/dot_general | solution.py:22
  119.0 65.2 %all-gather.3.cloned.1.call-done = f32[128,8192]{1,0:T(8,128)} async-done(((f32[128,512]{1,0:T(8,128)}), f32[128,8192]{1,0:T(8,128)}) %all-gather.3.cloned.1.call-update) | async-done | bytes 4194320 | tf_op jit(solution)/shard_map/all_gather | solution.py:33
  184.2 0.0 copy-done.3
  184.2 0.0 copy-done.5
  184.2 13.3 %select_select_fusion = (f32[128,256]{1,0:T(8,128)S(1)}, f32[128,256]{1,0:T(8,128)S(1)}) fusion(s32[128,256]{1,0:T(8,128)S(1)} %copy-done.3, f32[128,256]{1,0:T(8,128)S(1)} %fusion, f32[256]{0:T(256)S(1)} %copy-done.5, f32[128,8192]{1,0:T(8,128)} %all-gather.3.cloned.1.call-done, f32[256,8192]{1,0:T(8,128)} %param.17), kind=kOutput, calls=%fused_computation.23 | convolution fusion | flops 3221618688 | bytes 13108224 | tf_op jit(solution)/shard_map/dot_general | solution.py:21
  197.6 1.6 gather_fusion.3
  199.2 1.6 gather_fusion.6
  200.7 0.4 fusion.4
  201.2 18.5 %convolution_bitcast_fusion = f32[8192,512]{0,1:T(8,128)} fusion(f32[256,8192]{1,0:T(8,128)} %param.17, f32[512,256]{1,0:T(8,128)S(1)} %get-tuple-element.7, f32[512,256]{1,0:T(8,128)S(1)} %gather_fusion.3, pred[512]{0:T(512)(128)(4,1)S(1)} %get-tuple-element.10), kind=kOutput, calls=%fused_computation.7 | convolution fusion | flops 12885164032 | bytes 26214912 | tf_op jit(solution)/shard_map/dot_general | solution.py:45
  219.7 0.0 copy-start.2
  219.7 0.0 reduce-scatter.2.cloned.1.call-update
  219.7 0.9 copy-done.2
  220.7 0.0 copy-start.1
  220.7 1.6 gather_fusion.4
  222.3 0.0 copy-done.1
  222.3 2.3 gather_fusion.5
  224.6 202.9 %reduce-scatter.2.cloned.1.call-done = f32[512,512]{0,1:T(8,128)} async-done(((f32[8192,512]{0,1:T(8,128)}), f32[512,512]{0,1:T(8,128)}) %reduce-scatter.2.cloned.1.call-update) | async-done | bytes 1048592 | tf_op jit(solution)/shard_map/reduce_scatter | solution.py:44
  427.5 2.0 fusion.3
  429.5 44.0 %psum.7 = f32[512]{0:T(512)} all-reduce(f32[512]{0:T(512)S(1)} %add_add_fusion), channel_id=1, replica_groups=mesh['spec'=16,'neuron'=16] {'neuron'}, use_global_device_ids=true, to_apply=%region_4.8 | all-reduce | flops 512 | bytes 4096 | tf_op jit(solution)/shard_map/psum | solution.py:53
  (5 shorter events, 0.0 us)
Async XLA Ops:
  7.2 44.7 %copy-start = (f32[1000,256]{1,0:T(8,128)S(1)}, f32[1000,256]{1,0:T(8,128)}, u32[]{:S(2)}) copy-start(f32[1000,256]{1,0:T(8,128)} %param.19) | copy-start | bytes 3072004
  7.2 48.7 %copy-start.4 = (s32[512]{0:T(512)S(1)}, s32[512]{0:T(512)}, u32[]{:S(2)}) copy-start(s32[512]{0:T(512)} %param.22) | copy-start | bytes 6148
  7.2 98.8 %all-gather.5.cloned.1.call-start = ((), (), s32[]{:S(2)}) async-start(), calls=%async_computation.2 | async-start | bytes 4456448 | tf_op jit(solution)/shard_map/all_gather | solution.py:34
  27.8 156.4 %all-gather.3.cloned.1.call-start = ((), (), s32[]{:S(2)}) async-start(), calls=%async_computation.1 | async-start | bytes 4456448 | tf_op jit(solution)/shard_map/all_gather | solution.py:33
  47.0 380.6 %reduce-scatter.2.cloned.1.call-start = ((), (), s32[]{:S(2)}) async-start(), calls=%async_computation.3 | async-start | bytes 17825792 | tf_op jit(solution)/shard_map/reduce_scatter | solution.py:44
  54.1 130.1 %copy-start.3 = (s32[128,256]{1,0:T(8,128)S(1)}, s32[128,256]{1,0:T(8,128)}, u32[]{:S(2)}) copy-start(s32[128,256]{1,0:T(8,128)} %param.20) | copy-start | bytes 393220
  54.1 130.1 %copy-start.5 = (f32[256]{0:T(256)S(1)}, f32[256]{0:T(256)}, u32[]{:S(2)}) copy-start(f32[256]{0:T(256)} %param.18) | copy-start | bytes 3076
  219.7 0.9 copy-start.2
  220.7 1.6 copy-start.1
Sparse Core Ops, SparseCore 0:
  27.9 78.0 all-gather.4
  108.4 75.7 all-gather.2
  219.9 207.6 reduce-scatter.1
where the time goes:
time: 480 us
  waiting for transfers between devices  318 us (66%)
  blocking collectives  83.7 us (17%)
  matrix products  44.9 us (9%)
  local copies, waits for them, and re-layouts  14.8 us (3%)
  between operations  13.9 us (3%)
    reduce_scatter x1, waiting for transfers between devices, local(): lax.psum_scatter(lax.dot_general(weight, scaled, (((0,), (1,)), ((), ()))...  203 us
    all_gather x1, waiting for transfers between devices, local(): lax.all_gather(center_all, 'neuron', axis=1, tiled=True)  65.2 us
    all_gather x1, waiting for transfers between devices, local(): lax.all_gather(radius_all, 'neuron', axis=1, tiled=True)  50.1 us
    psum x1, blocking collectives, local(): margin_bounds = lax.psum(input_part + relax_part, 'neuron')  44 us
    all_gather x1, blocking collectives, local(): lax.all_gather(radius, 'spec', axis=0, tiled=True)  20.5 us
    all_gather x1, blocking collectives, local(): lax.all_gather(center, 'spec', axis=0, tiled=True)  19.1 us
    dot_general x1, matrix products, local(): lax.dot_general(weight, scaled, (((0,), (1,)), ((), ())), precision=highest)  18.5 us
    dot_general x1, matrix products, interval(): lax.dot_general(center_full, weight, dims, precision=highest) + bias  13.3 us
  transfers between devices with their start and end apart: 3, of which 3 were waited for; matrix products, arithmetic and copies ran while one was open for 5% of the time, Pallas kernels for 0%

commit v1 on v0

--- a/solution.py
+++ b/solution.py
@@ -30,7 +30,10 @@
         lax.all_gather(radius, "spec", axis=0, tiled=True),
     )
     center_full, radius_full = (
-        lax.all_gather(center_all, "neuron", axis=1, tiled=True),
+        jnp.concatenate(
+            lax.all_to_all(jnp.stack([center_all] * lax.axis_size("neuron")), "neuron", 0, 0),
+            axis=1,
+        ),
         lax.all_gather(radius_all, "neuron", axis=1, tiled=True),
     )
     slopes_all, offsets_all = interval(center_full, radius_full, weight, bias, masks)

time: 480 us -> 497 us (1.035)
  starting transfers between devices: 0.12 us -> 11.1 us
  waiting for transfers between devices: 318 us -> 325 us
    all_gather x1, waiting for transfers between devices: 50.1 us -> 118 us  [local(): lax.all_gather(radius_all, 'neuron', axis=1, tiled=True)]
    all_gather x1 -> x0, waiting for transfers between devices: 65.2 us -> none  [local(): lax.all_gather(center_all, 'neuron', axis=1, tiled=True)]
    all_to_all x0 -> x1, starting transfers between devices: none -> 11 us  [local(): lax.all_to_all(jnp.stack([center_all] * lax.axis_size('neuron')), 'neuron...]
  transfers between devices with their start and end apart: 3 -> 3, of which waited for: 3 -> 2; matrix products, arithmetic and copies ran while one was open for 5% -> 5% of each run, Pallas kernels for 0% -> 0%
where the time goes in v1:
time: 497 us; the launch traced here: 496 us
  waiting for transfers between devices  325 us (65%)
  blocking collectives  81.7 us (16%)
  matrix products  43.2 us (9%)
  local copies, waits for them, and re-layouts  16.9 us (3%)
  between operations  14.3 us (3%)
  starting transfers between devices  11.1 us (2%)
    reduce_scatter x1, waiting for transfers between devices, local(): lax.psum_scatter(lax.dot_general(weight, scaled, (((0,), (1,)), ((), ()))...  207 us
    all_gather x1, waiting for transfers between devices, local(): lax.all_gather(radius_all, 'neuron', axis=1, tiled=True)  118 us
    psum x1, blocking collectives, local(): margin_bounds = lax.psum(input_part + relax_part, 'neuron')  43.6 us
    all_gather x1, blocking collectives, local(): lax.all_gather(radius, 'spec', axis=0, tiled=True)  20.5 us
    dot_general x1, matrix products, local(): lax.dot_general(weight, scaled, (((0,), (1,)), ((), ())), precision=highest)  18.5 us
    all_gather x1, blocking collectives, local(): lax.all_gather(center, 'spec', axis=0, tiled=True)  17.5 us
    dot_general x1, matrix products, interval(): lax.dot_general(radius_full, jnp.abs(weight), dims, precision=highest)  13 us
    dot_general x1, matrix products, interval(): lax.dot_general(center_full, weight, dims, precision=highest) + bias  11.6 us
  transfers between devices with their start and end apart: 3, of which 2 were waited for; matrix products, arithmetic and copies ran while one was open for 5% of the time, Pallas kernels for 0%

profile of v1, /device:TPU:2, one launch (start us, length us, event | category | flops | bytes accessed | tf_op | source)
XLA Modules:
  0.0 495.9 jit_solution(4335231327333084808)
XLA Ops:
  7.2 0.0 copy-start
  7.2 0.0 copy-start.4
  7.2 0.0 copy-start.1
  7.2 0.0 all-gather.2.cloned.1.call-start
  7.2 20.5 %all_gather.10 = f32[128,512]{1,0:T(8,128)} all-gather(f32[8,512]{1,0:T(8,128)} %param.16), channel_id=1, replica_groups=mesh['spec'=16,'neuron'=16] {'spec'}, dimensions={0}, use_global_device_ids=true | all-gather | bytes 278528 | tf_op jit(solution)/shard_map/all_gather | solution.py:30
  27.8 0.0 all-gather.2.cloned.1.call-update
  27.8 17.5 %all_gather.9 = f32[128,512]{1,0:T(8,128)S(1)} all-gather(f32[8,512]{1,0:T(8,128)} %param.15), channel_id=1, replica_groups=mesh['spec'=16,'neuron'=16] {'spec'}, dimensions={0}, use_global_device_ids=true | all-gather | bytes 278528 | tf_op jit(solution)/shard_map/all_gather | solution.py:29
  45.3 0.1 copy.11
  45.5 2.4 stack.2
  47.8 0.0 copy-start.5
  47.8 11.0 %all-to-all-start = ((f32[16,128,512]{1,2,0:T(8,128)}), f32[16,128,512]{1,2,0:T(8,128)}, u32[]{:S(2)}, u32[]{:S(2)}) async-start(f32[16,128,512]{1,2,0:T(8,128)} %stack.2), calls=%async_computation | async-start | bytes 8388608 | tf_op jit(solution)/shard_map/all_to_all | solution.py:34
  58.9 0.0 reduce-scatter.2.cloned.1.call-start
  58.9 0.0 copy-done.4
  59.0 0.0 copy-done.1
  59.0 3.3 gather_fusion
  62.3 0.0 copy-done
  62.4 1.6 gather_fusion.1
  63.9 0.0 copy-done.5
  64.0 0.0 copy-start.3
  64.0 0.0 copy-start.6
  64.0 1.8 gather_fusion.2
  65.8 117.9 %all-gather.2.cloned.1.call-done = f32[128,8192]{1,0:T(8,128)} async-done(((f32[128,512]{1,0:T(8,128)}), f32[128,8192]{1,0:T(8,128)}) %all-gather.2.cloned.1.call-update) | async-done | bytes 4194320 | tf_op jit(solution)/shard_map/all_gather | solution.py:37
  183.6 13.0 %fusion = f32[128,256]{1,0:T(8,128)S(1)} fusion(f32[128,8192]{1,0:T(8,128)} %all-gather.2.cloned.1.call-done, f32[256,8192]{1,0:T(8,128)} %param.17), kind=kOutput, calls=%fused_computation.8 | convolution fusion | flops 3223322624 | bytes 12713984 | tf_op jit(solution)/shard_map/dot_general | solution.py:22
  196.6 0.0 all-to-all-done
  196.7 0.0 copy-done.3
  196.7 0.0 copy-done.6
  196.7 11.6 %select_select_fusion = (f32[128,256]{1,0:T(8,128)S(1)}, f32[128,256]{1,0:T(8,128)S(1)}) fusion(s32[128,256]{1,0:T(8,128)S(1)} %copy-done.3, f32[128,256]{1,0:T(8,128)S(1)} %fusion, f32[256]{0:T(256)S(1)} %copy-done.6, f32[128,8192]{0,1:T(8,128)} %bitcast.1, f32[256,8192]{1,0:T(8,128)} %param.17), kind=kOutput, calls=%fused_computation.23 | convolution fusion | flops 3221618688 | bytes 13108224 | tf_op jit(solution)/shard_map/dot_general | solution.py:21
  208.3 1.6 gather_fusion.3
  209.9 2.2 gather_fusion.6
  212.1 1.5 fusion.4
  213.6 18.5 %convolution_bitcast_fusion = f32[8192,512]{0,1:T(8,128)} fusion(f32[256,8192]{1,0:T(8,128)} %param.17, f32[512,256]{1,0:T(8,128)S(1)} %get-tuple-element.7, f32[512,256]{1,0:T(8,128)S(1)} %gather_fusion.3, pred[512]{0:T(512)(128)(4,1)S(1)} %get-tuple-element.10), kind=kOutput, calls=%fused_computation.7 | convolution fusion | flops 12885164032 | bytes 26214912 | tf_op jit(solution)/shard_map/dot_general | solution.py:48
  232.2 0.0 reduce-scatter.2.cloned.1.call-update
  232.2 0.0 copy-start.2
  232.2 1.6 gather_fusion.4
  233.8 0.0 copy-done.2
  233.8 2.3 gather_fusion.5
  236.2 207.3 %reduce-scatter.2.cloned.1.call-done = f32[512,512]{0,1:T(8,128)} async-done(((f32[8192,512]{0,1:T(8,128)}), f32[512,512]{0,1:T(8,128)}) %reduce-scatter.2.cloned.1.call-update) | async-done | bytes 1048592 | tf_op jit(solution)/shard_map/reduce_scatter | solution.py:47
  443.4 2.0 fusion.3
  445.4 43.6 %psum.7 = f32[512]{0:T(512)} all-reduce(f32[512]{0:T(512)S(1)} %add_add_fusion), channel_id=1, replica_groups=mesh['spec'=16,'neuron'=16] {'neuron'}, use_global_device_ids=true, to_apply=%region_4.8 | all-reduce | flops 512 | bytes 4096 | tf_op jit(solution)/shard_map/psum | solution.py:56
  (8 shorter events, 0.1 us)
Async XLA Ops:
  7.2 55.2 %copy-start = (f32[1000,256]{1,0:T(8,128)S(1)}, f32[1000,256]{1,0:T(8,128)}, u32[]{:S(2)}) copy-start(f32[1000,256]{1,0:T(8,128)} %param.19) | copy-start | bytes 3072004
  7.2 51.7 %copy-start.4 = (s32[512]{0:T(512)S(1)}, s32[512]{0:T(512)}, u32[]{:S(2)}) copy-start(s32[512]{0:T(512)} %param.23) | copy-start | bytes 6148
  7.2 51.8 %copy-start.1 = (s32[128]{0:T(128)S(1)}, s32[128]{0:T(128)}, u32[]{:S(2)}) copy-start(s32[128]{0:T(128)} %param.21) | copy-start | bytes 1540
  7.2 176.4 %all-gather.2.cloned.1.call-start = ((), (), s32[]{:S(2)}) async-start(), calls=%async_computation.2 | async-start | bytes 4456448 | tf_op jit(solution)/shard_map/all_gather | solution.py:37
  47.8 16.1 %copy-start.5 = (s32[512]{0:T(512)S(1)}, s32[512]{0:T(512)}, u32[]{:S(2)}) copy-start(s32[512]{0:T(512)} %param.22) | copy-start | bytes 6148
  47.8 148.8 %all-to-all-start = ((f32[16,128,512]{1,2,0:T(8,128)}), f32[16,128,512]{1,2,0:T(8,128)}, u32[]{:S(2)}, u32[]{:S(2)}) async-start(f32[16,128,512]{1,2,0:T(8,128)} %stack.2), calls=%async_computation | async-start | bytes 8388608 | tf_op jit(solution)/shard_map/all_to_all | solution.py:34
  58.9 384.5 %reduce-scatter.2.cloned.1.call-start = ((), (), s32[]{:S(2)}) async-start(), calls=%async_computation.3 | async-start | bytes 17825792 | tf_op jit(solution)/shard_map/reduce_scatter | solution.py:47
  64.0 132.7 %copy-start.3 = (s32[128,256]{1,0:T(8,128)S(1)}, s32[128,256]{1,0:T(8,128)}, u32[]{:S(2)}) copy-start(s32[128,256]{1,0:T(8,128)} %param.20) | copy-start | bytes 393220
  64.0 132.7 %copy-start.6 = (f32[256]{0:T(256)S(1)}, f32[256]{0:T(256)}, u32[]{:S(2)}) copy-start(f32[256]{0:T(256)} %param.18) | copy-start | bytes 3076
  232.2 1.6 copy-start.2
Sparse Core Ops, SparseCore 0:
  27.9 155.6 all-gather.1
  232.3 211.0 reduce-scatter.1
